TPU v7x, 512 devices: a whole 4x4x16 slice. The times are simulated.
512 devices in a mesh: vox: 8 (over x, z_hi), row: 16 (over z_lo, core), wl: 4 (over y).
Axes of the slice: x: 4, y: 4, z: 16 (z_hi: 2, z_lo: 8; z = z_hi * 8 + z_lo), core: 2. Of those that a mesh axis runs over, the one named last changes fastest.
Arguments:
- jacobian: bfloat16 [8192, 5120], P(('row', 'wl'), 'vox'), may hold values from -0.078125 to 0.078125
- extinction: float32 [4, 2], replicated, may hold values from 0.3 to 3
- prior_var: float32 [2, 5120], P(None, 'vox'), may hold values from 0.1 to 10
Outputs:
- gram: float32 [8192, 8192], P(('row', 'wl'), 'vox')
All inputs are finite; a program needn't handle non-finite values.
Results may differ from a plain program's by a relative error of at most 0.005.
Values may be sent and summed in bfloat16 or wider, within the bound.
A program may use at most 128 MiB of HBM per device.

v0:
```python
import jax
import jax.numpy as jnp
from jax import lax
from jax.sharding import PartitionSpec as P


def spectral_table(extinction, prior_var, wave_index):
    coeff = lax.dynamic_index_in_dim(extinction, wave_index, 0, keepdims=True)
    return jnp.dot(extinction * coeff, prior_var, precision=lax.Precision.HIGHEST)


def weigh_rows(portion, table, tile_rows):
    count = portion.shape[0]
    waves = jnp.arange(count, dtype=jnp.int32) // tile_rows % table.shape[0]
    onehot = (waves[:, None] == jnp.arange(table.shape[0], dtype=jnp.int32)[None, :]).astype(
        jnp.float32
    )
    weights = jnp.dot(onehot, table, precision=lax.Precision.HIGHEST)
    return portion.astype(jnp.float32) * weights


def contract(left_rows, right_rows):
    return lax.dot_general(
        left_rows.astype(jnp.float32),
        right_rows,
        (((1,), (1,)), ((), ())),
        precision=lax.Precision.HIGHEST,
        preferred_element_type=jnp.float32,
    )


def on_device(jacobian, extinction, prior_var):
    tile_rows = jacobian.shape[0]
    band_count = lax.axis_size("wl")
    waves_total = extinction.shape[0]
    own_block = lax.axis_index("row") * band_count + lax.axis_index("wl")
    own_table = spectral_table(extinction, prior_var, own_block % waves_total)
    portion = lax.all_gather(jacobian, ("row", "wl"), axis=0, tiled=True)
    count = portion.shape[0]
    empty = jnp.zeros((tile_rows, count), jnp.float32)
    terms = lax.cond(
        jnp.int32(0) < (own_block + 1) * tile_rows,
        lambda: contract(jacobian, weigh_rows(portion, own_table, tile_rows)),
        lambda: empty,
    )
    summed = lax.psum_scatter(terms, "vox", scatter_dimension=1, tiled=True)
    width = summed.shape[1]
    rows_global = own_block * tile_rows + jnp.arange(tile_rows, dtype=jnp.int32)
    cols_global = lax.axis_index("vox") * width + jnp.arange(width, dtype=jnp.int32)
    return jnp.where(cols_global[None, :] <= rows_global[:, None], summed, jnp.float32(0.0))


def solution(mesh):
    return jax.shard_map(
        on_device,
        mesh=mesh,
        in_specs=(P(("row", "wl"), "vox"), P(), P(None, "vox")),
        out_specs=P(("row", "wl"), "vox"),
        check_vma=False,
    )
```

profile of v0, /device:TPU:24, one launch (start us, length us, event | category | flops | bytes accessed | tf_op | source)
XLA Modules:
  0.0 469.8 jit_solution(4404956184555582500)
XLA Ops:
  6.5 0.0 copy-start
  6.5 0.0 all-gather.2.cloned.1.call-start
  6.5 0.7 all-gather.2.cloned.1.call-update
  7.3 0.0 reduce-scatter.2.cloned.1.call-start
  7.3 0.9 dynamic-slice_reduce_fusion
  8.2 0.0 copy-done
  8.2 0.9 fusion.12
  9.2 197.6 %all-gather.2.cloned.1.call-done = bf16[8192,640]{1,0:T(8,128)(2,1)} async-done(((bf16[128,640]{1,0:T(8,128)(2,1)}), bf16[8192,640]{1,0:T(8,128)(2,1)}) %all-gather.2.cloned.1.call-update) | async-done | bytes 10485776 | tf_op jit(solution)/shard_map/all_gather | solution.py:38
  206.7 31.0 %conditional.1 = (f32[128,8192]{0,1:T(8,128)}) conditional(s32[]{:T(128)} %convert_element_type.8, () %tuple.11, (bf16[8192,640]{1,0:T(8,128)(2,1)}, f32[4,640]{1,0:T(4,128)S(1)}, bf16[128,640]{1,0:T(8,128)(2,1)}) %tuple.12), branch_computations={%region_0.1_spmd, %region_1.2_spmd} | conditional | flops 8315396096 | bytes 57518116 | solution.py:41
  206.7 0.0 copy-start.1
  206.7 13.1 %fusion.6 = f32[8192,640]{1,0:T(8,128)} fusion(f32[4,640]{1,0:T(4,128)S(1)} %get-tuple-element.15, s32[8192]{0:T(1024)S(1)} %add_select_fusion), kind=kOutput, calls=%fused_computation.5 | convolution fusion | flops 251691008 | bytes 21014528 | tf_op jit(solution)/shard_map/cond/branch_1_fun/dot_general | solution.py:18
  219.9 0.0 copy-done.1
  219.9 17.8 %fusion.3 = f32[128,8192]{0,1:T(8,128)} fusion(bf16[128,640]{1,0:T(8,128)(2,1)S(1)} %copy-done.1, f32[8192,640]{1,0:T(8,128)} %fusion.6, bf16[8192,640]{1,0:T(8,128)(2,1)} %get-tuple-element.14), kind=kOutput, calls=%fused_computation.3 | convolution fusion | flops 8063549440 | bytes 35815424 | tf_op jit(solution)/shard_map/cond/branch_1_fun/dot_general | solution.py:23
  237.7 5.6 %copy.5 = f32[128,8192]{1,0:T(8,128)} copy(f32[128,8192]{0,1:T(8,128)} %get-tuple-element.17) | data formatting | bytes 8388608 | tf_op jit(solution)/shard_map/cond | solution.py:41
  243.3 0.0 reduce-scatter.2.cloned.1.call-update
  243.4 217.7 %reduce-scatter.2.cloned.1.call-done = f32[128,1024]{1,0:T(8,128)} async-done(((f32[128,8192]{1,0:T(8,128)}), f32[128,1024]{1,0:T(8,128)}) %reduce-scatter.2.cloned.1.call-update) | async-done | bytes 524304 | tf_op jit(solution)/shard_map/reduce_scatter | solution.py:46
  461.0 1.9 compare_select_fusion
  (3 shorter events, 0.0 us)
Async XLA Ops:
  6.5 1.7 copy-start
  6.5 200.2 %all-gather.2.cloned.1.call-start = ((), (), s32[]{:S(2)}) async-start(), calls=%async_computation.1 | async-start | bytes 10649600 | tf_op jit(solution)/shard_map/all_gather | solution.py:38
  7.3 453.8 %reduce-scatter.2.cloned.1.call-start = ((), (), s32[]{:S(2)}) async-start(), calls=%async_computation.2 | async-start | bytes 4718592 | tf_op jit(solution)/shard_map/reduce_scatter | solution.py:46
  206.7 13.1 %copy-start.1 = (bf16[128,640]{1,0:T(8,128)(2,1)S(1)}, bf16[128,640]{1,0:T(8,128)(2,1)}, u32[]{:S(2)}) copy-start(bf16[128,640]{1,0:T(8,128)(2,1)} %get-tuple-element.16) | copy-start | bytes 491524 | tf_op jit(solution)/shard_map/cond
Sparse Core Ops, SparseCore 0:
  9.4 197.2 all-gather.1
  243.5 217.5 reduce-scatter.1
where the time goes:
time: 470 us
  waiting for transfers between devices  416 us (89%)
  matrix products  31.9 us (7%)
  between operations  13.5 us (3%)
  local copies, waits for them, and re-layouts  6.51 us (1%)
    reduce_scatter x1, waiting for transfers between devices, on_device(): summed = lax.psum_scatter(terms, 'vox', scatter_dimension=1, tiled=True)  218 us
    all_gather x1, waiting for transfers between devices, on_device(): portion = lax.all_gather(jacobian, ('row', 'wl'), axis=0, tiled=True)  198 us
    dot_general x1, matrix products, contract(): lax.dot_general(left_rows.astype(jnp.float32), right_rows, (((1,), (1,)),...  17.8 us
    dot_general x1, matrix products, weigh_rows(): weights = jnp.dot(onehot, table, precision=lax.Precision.HIGHEST)  13.1 us
  transfers between devices with their start and end apart: 2, of which 2 were waited for; matrix products, arithmetic and copies ran while one was open for 0% of the time, Pallas kernels for 0%

commit v1 on v0

v1 whole, which is shorter than its diff:
```python
import functools
import jax
import jax.numpy as jnp
from jax import lax
from jax.experimental import pallas as pl
from jax.experimental.pallas import tpu as pltpu
from jax.sharding import PartitionSpec as P

MESH = pl.DeviceIdType.MESH
NT = (((1,), (1,)), ((), ()))


def rem(a, n):
    return lax.rem(a, jnp.int32(n))


def div(a, n):
    return lax.div(a, jnp.int32(n))


def kernel(
    pieces,
    j_ref, ext_ref, pri_ref, out_ref,
    zb, cb, rb, prx, sh, sl, part, ra, rx, fin, yb,
    zs, zr, cs, cr, ys, yr, as_, ar, xs, xr, fs, fr, ps, pr,
):
    rows, vox = j_ref.shape
    step = rows // pieces
    half_rows = rows // 2
    v = lax.axis_index("vox")
    r = lax.axis_index("row")
    y = lax.axis_index("wl")
    x, h = div(v, 2), rem(v, 2)
    i, c = div(r, 2), rem(r, 2)
    z = h * 8 + i
    kind = rem(i + h, 2)

    def at(x_=None, z_=None, y_=None, c_=None):
        x_ = x if x_ is None else x_
        z_ = z if z_ is None else z_
        y_ = y if y_ is None else y_
        c_ = c if c_ is None else c_
        return {"vox": x_ * 2 + div(z_, 8), "row": rem(z_, 8) * 2 + c_, "wl": y_}

    x_next, x_prev = at(x_=rem(x + 1, 4)), at(x_=rem(x + 3, 4))
    y_next, y_prev, y_far = at(y_=rem(y + 1, 4)), at(y_=rem(y + 3, 4)), at(y_=rem(y + 2, 4))
    z_next, z_prev, z_far = at(z_=rem(z + 1, 16)), at(z_=rem(z + 15, 16)), at(z_=rem(z + 8, 16))
    other = at(c_=1 - c)
    z_to = (z_next, z_prev)

    barrier = pltpu.get_barrier_semaphore()
    partners = (x_next, x_prev, y_next, y_prev, y_far, z_next, z_prev, z_far, other)
    for device in partners:
        pl.semaphore_signal(barrier, inc=1, device_id=device, device_id_type=MESH)
    pl.semaphore_wait(barrier, len(partners))

    def send(src, dst, ssem, rsem, device):
        return pltpu.make_async_remote_copy(
            src_ref=src, dst_ref=dst, send_sem=ssem, recv_sem=rsem,
            device_id=device, device_id_type=MESH,
        )

    def kind_at(way, d):
        s = rem(z + 16 - d, 16) if way == 0 else rem(z + d, 16)
        return rem(div(s, 8) + s, 2)

    def z_copy(way, d, p, src):
        cut = pl.ds(p * step, step)
        return send(
            src.at[cut, :], zb.at[way, d, cut, :], zs.at[way, d, p], zr.at[way, d, p], z_to[way]
        )

    def target(delta):
        return rem(div(i - delta - h, 2) + 4 - x, 4)

    def c_copy(where, src, dx):
        return send(src, cb.at[dx, where], cs.at[where, dx], cr.at[where, dx], other)

    def y_copy(where, q, s, src):
        cut = pl.ds(q * half_rows, half_rows)
        return send(
            src.at[cut, :], rb.at[s - 1, where, cut, :],
            ys.at[where, q, s - 1], yr.at[where, q, s - 1],
            y_prev if s == 3 or (s == 2 and q == 1) else y_next,
        )

    def y_relay(where, q):
        s = 1 if q == 0 else 3
        y_copy(where, q, s, rb.at[s - 1, where]).wait_recv()
        y_copy(where, q, 2, rb.at[s - 1, where]).start()

    p_copy = send(pri_ref, prx, ps, pr, z_far)
    for way in (0, 1):
        @pl.when(kind == way)
        def _():
            for p in range(pieces):
                z_copy(way, 1, p, j_ref).start()
    for q in (0, 1):
        for s in (1, 3):
            y_copy(0, q, s, j_ref).start()
    p_copy.start()

    @pl.when(kind == 0)
    def _():
        c_copy(0, j_ref, target(0)).start()
        zb[0, 0] = j_ref[...]

    def hop(d, carry):
        for way in (0, 1):
            @pl.when(kind_at(way, d) == way)
            def _():
                for p in range(pieces):
                    z_copy(way, d, p, zb.at[way, d]).wait_recv()
                    @pl.when(d < 8)
                    def _():
                        z_copy(way, d + 1, p, zb.at[way, d]).start()
                    if (p + 1) % (pieces // 2) == 0:
                        q = (p + 1) // (pieces // 2) - 1
                        @pl.when(d == 8)
                        def _():
                            y_copy(1, q, 1, zb.at[way, d]).start()
                            y_copy(1, q, 3, zb.at[way, d]).start()
                delta = d if way == 0 else 8 - d
                @pl.when(delta <= i)
                def _():
                    c_copy(way, zb.at[way, d], target(delta)).start()

        @pl.when(d == 3)
        def _():
            y_relay(0, 0)
            y_relay(0, 1)
        return carry

    lax.fori_loop(1, 9, hop, 0)

    def weight(pri, a):
        w0 = ext_ref[a, 0] * ext_ref[y, 0]
        w1 = ext_ref[a, 1] * ext_ref[y, 1]
        return pri[0:1, :] * w0 + pri[1:2, :] * w1

    def scale(where, s, src, pri):
        value = src.astype(jnp.float32) * weight(pri, rem(y + 4 - s, 4))
        high = value.astype(jnp.bfloat16)
        cut = pl.ds(s * rows, rows)
        sh[where, cut, :] = high
        sl[where, cut, :] = (value - high.astype(jnp.float32)).astype(jnp.bfloat16)

    def active(dx):
        return rem(x + dx, 4) * 2 + h <= i

    def columns(where, dx):
        j = rem(x + dx, 4) * 2 + h
        delta = i - j
        own = zb[0, delta] if where == 0 else zb[1, 8 - delta]
        return jnp.concatenate([own, cb[dx, where]], axis=0)

    def product(where, dx):
        cols = columns(where, dx)
        return lax.dot_general(
            sh[where], cols, NT, preferred_element_type=jnp.float32
        ) + lax.dot_general(sl[where], cols, NT, preferred_element_type=jnp.float32)

    for q in (0, 1):
        y_copy(0, q, 1 if q == 1 else 3, j_ref).wait_recv()
        y_copy(0, q, 2, j_ref).wait_recv()
    scale(0, 0, j_ref[...], pri_ref[...])
    for s in (1, 2, 3):
        scale(0, s, rb[s - 1, 0], pri_ref[...])
    for dx in (2, 1, 3, 0):
        @pl.when(active(dx))
        def _():
            c_copy(0, j_ref, dx).wait_recv()
            part[dx] = product(0, dx)

    y_relay(1, 0)
    y_relay(1, 1)
    p_copy.wait_recv()
    scale(1, 0, zb[1 - kind, 8], prx[...])
    y_copy(1, 1, 1, j_ref).wait_recv()
    scale(1, 1, rb[0, 1], prx[...])
    y_copy(1, 0, 3, j_ref).wait_recv()
    scale(1, 3, rb[2, 1], prx[...])
    for q in (0, 1):
        y_copy(1, q, 2, j_ref).wait_recv()
    scale(1, 2, rb[1, 1], prx[...])

    wide = rows * 2

    def a_copy(k):
        return send(
            part.at[2, pl.ds(k * wide, wide), :], ra.at[k], as_.at[k], ar.at[k],
            x_next if k == 0 else x_prev,
        )

    def x_copy(k, q):
        cut = pl.ds(q * wide, wide)
        return send(
            part.at[1 if k == 0 else 3, cut, :], rx.at[k, cut, :], xs.at[k, q], xr.at[k, q],
            x_next if k == 0 else x_prev,
        )

    for dx in (2, 1, 3, 0):
        @pl.when(active(dx))
        def _():
            c_copy(1, j_ref, dx).wait_recv()
            part[dx] = part[dx] + product(1, dx)
            if dx == 2:
                a_copy(0).start()
                a_copy(1).start()
            if dx == 1:
                x_copy(0, 1).start()
            if dx == 3:
                x_copy(1, 0).start()
    for k, dx in ((0, 1), (1, 3)):
        @pl.when(active(dx))
        def _():
            a_copy(k).wait_recv()
            cut = pl.ds(k * wide, wide)
            part[dx, cut, :] = part[dx, cut, :] + ra[k]
            x_copy(k, k).start()

    def f_copy(s):
        cut = pl.ds(s * rows, rows)
        device = {1: y_prev, 2: y_far, 3: y_next}[s]
        return send(fin.at[cut, :], yb.at[s - 1], fs.at[s - 1], fr.at[s - 1], device)

    j_own = x * 2 + h
    mine = j_own <= i

    @pl.when(mine)
    def _():
        for q in (0, 1):
            x_copy(0, q).wait_recv()
            x_copy(1, q).wait_recv()
            cut = pl.ds(q * wide, wide)
            fin[cut, :] = part[0, cut, :] + rx[0, cut, :] + rx[1, cut, :]
            for s in ((1,) if q == 0 else (2, 3)):
                f_copy(s).start()

        def place(s, value):
            source = rem(y + s, 4)
            row = ((i * 2 + c) * 4 + y) * rows + lax.broadcasted_iota(jnp.int32, (rows, rows), 0)
            lane = lax.broadcasted_iota(jnp.int32, (rows, rows), 1)
            for k in (0, 1):
                block = (c if k == 0 else 1 - c) * 4 + source
                col = j_own * (rows * 8) + block * rows + lane
                piece = value[:, k * rows:(k + 1) * rows]
                out_ref[:, pl.ds(pl.multiple_of(block * rows, rows), rows)] = jnp.where(
                    col <= row, piece, 0.0
                )

        place(0, fin[0:rows, :])
        for s in (1, 3, 2):
            f_copy(s).wait_recv()
            place(s, yb[s - 1])

    @pl.when(j_own > i)
    def _():
        out_ref[...] = jnp.zeros_like(out_ref)

    p_copy.wait_send()

    def drain(d, carry):
        for way in (0, 1):
            @pl.when(kind_at(way, d - 1) == way)
            def _():
                for p in range(pieces):
                    z_copy(way, d, p, zb.at[way, d]).wait_send()
        return carry

    lax.fori_loop(1, 9, drain, 0)
    for where in (0, 1):
        for q in (0, 1):
            for s in (1, 2, 3):
                y_copy(where, q, s, j_ref).wait_send()
    for dx in range(4):
        @pl.when(active(dx))
        def _():
            for where in (0, 1):
                c_copy(where, j_ref, dx).wait_send()
            if dx == 2:
                a_copy(0).wait_send()
                a_copy(1).wait_send()
            if dx == 1 or dx == 3:
                for q in (0, 1):
                    x_copy(0 if dx == 1 else 1, q).wait_send()

    @pl.when(mine)
    def _():
        for s in (1, 2, 3):
            f_copy(s).wait_send()


def on_device(pieces, jacobian, extinction, prior_var):
    rows, vox = jacobian.shape
    width = rows * 8
    dma = pltpu.SemaphoreType.DMA
    vmem = pltpu.VMEM
    f32, bf16 = jnp.float32, jnp.bfloat16
    return pl.pallas_call(
        functools.partial(kernel, pieces),
        out_shape=jax.ShapeDtypeStruct((rows, width), f32),
        in_specs=[
            pl.BlockSpec(memory_space=pltpu.VMEM),
            pl.BlockSpec(memory_space=pltpu.SMEM),
            pl.BlockSpec(memory_space=pltpu.VMEM),
        ],
        out_specs=pl.BlockSpec(memory_space=pltpu.VMEM),
        scratch_shapes=[
            vmem((2, 9, rows, vox), bf16),
            vmem((4, 2, rows, vox), bf16),
            vmem((3, 2, rows, vox), bf16),
            vmem((2, vox), f32),
            vmem((2, rows * 4, vox), bf16),
            vmem((2, rows * 4, vox), bf16),
            vmem((4, rows * 4, rows * 2), f32),
            vmem((2, rows * 2, rows * 2), f32),
            vmem((2, rows * 4, rows * 2), f32),
            vmem((rows * 4, rows * 2), f32),
            vmem((3, rows, rows * 2), f32),
            dma((2, 9, pieces)), dma((2, 9, pieces)),
            dma((2, 4)), dma((2, 4)),
            dma((2, 2, 3)), dma((2, 2, 3)),
            dma((2,)), dma((2,)),
            dma((2, 2)), dma((2, 2)),
            dma((3,)), dma((3,)),
            dma, dma,
        ],
        compiler_params=pltpu.CompilerParams(
            collective_id=0, has_side_effects=True, vmem_limit_bytes=48 * 2**20
        ),
    )(jacobian, extinction, prior_var)


def solution(mesh):
    return jax.shard_map(
        functools.partial(on_device, 4),
        mesh=mesh,
        in_specs=(P(("row", "wl"), "vox"), P(), P(None, "vox")),
        out_specs=P(("row", "wl"), "vox"),
        check_vma=False,
    )
```

time: 470 us -> 80.5 us (0.17)
  the two profiles are of different devices: /device:TPU:24 before, /device:TPU:64 now
where the time goes in v1:
time: 80.5 us; the launch traced here: 80.3 us
  Pallas kernels  77.1 us (96%)
  local copies, waits for them, and re-layouts  3.16 us (4%)
    pallas_call x1, Pallas kernels, on_device(): pl.pallas_call(functools.partial(kernel, pieces), out_shape=jax.ShapeDtyp...  77.1 us
    unnamed x6, local copies, waits for them, and re-layouts  3.16 us

profile of v1, /device:TPU:64, one launch (start us, length us, event | category | flops | bytes accessed | tf_op | source)
XLA Modules:
  0.0 80.3 jit_solution(8090973841090741657)
XLA Ops:
  0.0 0.8 copy.4.ext_ref
  0.8 0.0 copy-start
  0.8 0.9 %copy-done = bf16[128,640]{1,0:T(8,128)(2,1)S(1)} copy-done((bf16[128,640]{1,0:T(8,128)(2,1)S(1)}, bf16[128,640]{1,0:T(8,128)(2,1)}, u32[]{:S(2)}) %copy-start) | copy-done | bytes 163864
  1.7 0.0 copy-start.1
  1.7 0.7 copy-done.1
  2.4 77.1 %shard_map.37 = f32[128,1024]{1,0:T(8,128)S(1)} custom-call(bf16[128,640]{1,0:T(8,128)(2,1)S(1)} %copy-done, f32[4,2]{1,0:T(4,128)S(1)} %copy.4.ext_ref, f32[2,640]{1,0:T(2,128)S(1)} %copy-done.1), custom_call_target="tpu_custom_call" | custom-call | tf_op jit(solution)/shard_map/pallas_call | solution.py:300
  79.5 0.8 copy.6
Async XLA Ops:
  0.8 0.9 %copy-start = (bf16[128,640]{1,0:T(8,128)(2,1)S(1)}, bf16[128,640]{1,0:T(8,128)(2,1)}, u32[]{:S(2)}) copy-start(bf16[128,640]{1,0:T(8,128)(2,1)} %j_ref.1) | copy-start | bytes 491524
  1.7 0.7 copy-start.1

commit v2 on v1

v2 whole, which is shorter than its diff:
```python
import functools
import jax
import jax.numpy as jnp
from jax import lax
from jax.experimental import pallas as pl
from jax.experimental.pallas import tpu as pltpu
from jax.sharding import PartitionSpec as P

MESH = pl.DeviceIdType.MESH
NT = (((1,), (1,)), ((), ()))


def rem(a, n):
    return lax.rem(a, jnp.int32(n))


def div(a, n):
    return lax.div(a, jnp.int32(n))


def kernel(
    pieces,
    j_ref, ext_ref, pri_ref, out_ref,
    zb, cb, rb, ext, pri, tab, sh, sl, part, ra, rx, fin, yb, fb,
    zs, zr, cs, cr, ys, yr, as_, ar, xs, xr, fs, fr, gs, gr, ps, pr, ls,
):
    rows, vox = j_ref.shape
    step = rows // pieces
    half_rows = rows // 2
    v = lax.axis_index("vox")
    r = lax.axis_index("row")
    y = lax.axis_index("wl")
    x, h = div(v, 2), rem(v, 2)
    i, c = div(r, 2), rem(r, 2)
    z = h * 8 + i
    role = rem(i + h, 2)
    kind = rem(i + h + div(i, 7) * c, 2)

    def at(x_=None, z_=None, y_=None, c_=None):
        x_ = x if x_ is None else x_
        z_ = z if z_ is None else z_
        y_ = y if y_ is None else y_
        c_ = c if c_ is None else c_
        return {"vox": x_ * 2 + div(z_, 8), "row": rem(z_, 8) * 2 + c_, "wl": y_}

    x_next, x_prev = at(x_=rem(x + 1, 4)), at(x_=rem(x + 3, 4))
    y_next, y_prev = at(y_=rem(y + 1, 4)), at(y_=rem(y + 3, 4))
    z_next, z_prev = at(z_=rem(z + 1, 16)), at(z_=rem(z + 15, 16))
    z_up, z_down = at(z_=rem(z + 4, 16)), at(z_=rem(z + 12, 16))
    other = at(c_=1 - c)

    barrier = pltpu.get_barrier_semaphore()
    partners = (z_up, z_down, z_next, z_prev, y_next, y_prev, x_next, x_prev, other)
    for device in partners:
        pl.semaphore_signal(barrier, inc=1, device_id=device, device_id_type=MESH)
    loads = [
        pltpu.make_async_copy(src, dst, ls.at[k])
        for k, (src, dst) in enumerate(((j_ref, zb.at[0, 0]), (ext_ref, ext), (pri_ref, pri.at[0])))
    ]
    for load in loads:
        load.start()
    loads[0].wait()
    pl.semaphore_wait(barrier, len(partners))

    def send(src, dst, ssem, rsem, device):
        return pltpu.make_async_remote_copy(
            src_ref=src, dst_ref=dst, send_sem=ssem, recv_sem=rsem,
            device_id=device, device_id_type=MESH,
        )

    def source(way, d):
        s = rem(z + 16 - d, 16) if way == 0 else rem(z + d, 16)
        place = rem(s, 8)
        return rem(div(s, 8) + place + div(place, 7) * c, 2)

    def has(way, d):
        return source(way, d) == way

    def sends(way, d):
        return source(way, d - 1) == way

    def z_copy(way, d, p):
        cut = pl.ds(p * step, step)
        src = zb.at[0, 0] if d == 1 else zb.at[way, d - 1]
        device = z_next if way == 0 else z_prev
        return send(
            src.at[cut, :], zb.at[way, d, cut, :], zs.at[way, d, p], zr.at[way, d, p], device
        )

    def target(delta):
        return rem(div(i - delta - h, 2) + 4 - x, 4)

    def c_copy(where, src, dx):
        return send(src, cb.at[dx, where], cs.at[where, dx], cr.at[where, dx], other)

    def y_copy(where, q, s, src):
        cut = pl.ds(q * half_rows, half_rows)
        return send(
            src.at[cut, :], rb.at[s - 1, where, cut, :],
            ys.at[where, q, s - 1], yr.at[where, q, s - 1],
            y_prev if s == 3 or (s == 2 and q == 1) else y_next,
        )

    def y_relay(where, q):
        s = 1 if q == 0 else 3
        y_copy(where, q, s, rb.at[s - 1, where]).wait_recv()
        y_copy(where, q, 2, rb.at[s - 1, where]).start()

    def p_copy(k):
        return send(pri_ref if k == 0 else pri.at[1], pri.at[k + 1], ps.at[k], pr.at[k], z_up)

    def start_z(way, d, p):
        @pl.when(sends(way, d))
        def _():
            z_copy(way, d, p).start()

    for p in range(pieces):
        start_z(0, 1, p)
        start_z(1, 1, p)
    p_copy(0).start()
    for q in (0, 1):
        for s in (1, 3):
            y_copy(0, q, s, zb.at[0, 0]).start()

    @pl.when(role == 0)
    def _():
        c_copy(0, zb.at[0, 0], target(0)).start()

    def take(way, d):
        @pl.when(has(way, d))
        def _():
            for p in range(pieces):
                z_copy(way, d, p).wait_recv()
                if d < 8:
                    z_copy(way, d + 1, p).start()
                if d == 8 and (p + 1) % (pieces // 2) == 0:
                    q = (p + 1) // (pieces // 2) - 1
                    y_copy(1, q, 1, zb.at[way, d]).start()
                    y_copy(1, q, 3, zb.at[way, d]).start()
            if d < 8:
                delta = d if way == 0 else 8 - d

                @pl.when((delta <= i) & (rem(i + h + delta, 2) == 0))
                def _():
                    c_copy(way, zb.at[way, d], target(delta)).start()
            else:
                @pl.when(role == 0)
                def _():
                    c_copy(1, zb.at[way, d], target(0)).start()

    for way, d in ((0, 1), (1, 1), (0, 2), (1, 2), (0, 3), (1, 3)):
        take(way, d)
    y_relay(0, 0)
    y_relay(0, 1)
    p_copy(0).wait_recv()
    p_copy(1).start()
    for way, d in ((0, 4), (1, 4), (0, 5), (1, 5)):
        take(way, d)

    def weigh(where):
        both = ext[...] * ext[pl.ds(y, 1), :]
        own = pri[where * 2]
        tab[...] = both[:, 0:1] * own[0:1, :] + both[:, 1:2] * own[1:2, :]

    def scale(where, s, src):
        value = src.astype(jnp.float32) * tab[pl.ds(rem(y + 4 - s, 4), 1), :]
        high = value.astype(jnp.bfloat16)
        cut = pl.ds(s * rows, rows)
        sh[where, cut, :] = high
        sl[where, cut, :] = (value - high.astype(jnp.float32)).astype(jnp.bfloat16)

    for q in (0, 1):
        y_copy(0, q, 1 if q == 1 else 3, j_ref).wait_recv()
        y_copy(0, q, 2, j_ref).wait_recv()
    for load in loads[1:]:
        load.wait()
    weigh(0)
    scale(0, 0, zb[0, 0])
    for s in (1, 2, 3):
        scale(0, s, rb[s - 1, 0])
    for way, d in ((0, 6), (1, 6), (0, 7), (1, 7), (0, 8), (1, 8)):
        take(way, d)
    p_copy(1).wait_recv()
    weigh(1)
    scale(1, 0, zb[1 - kind, 8])

    def active(dx):
        return rem(x + dx, 4) * 2 + h <= i

    def columns(where, dx):
        j = rem(x + dx, 4) * 2 + h
        delta = i - j
        if where == 0:
            own = zb[0, delta]
        else:
            own = zb[jnp.where(delta == 0, 1 - kind, 1), 8 - delta]
        return jnp.concatenate([own, cb[dx, where]], axis=0)

    def half_product(where, cut, cols):
        return lax.dot_general(
            sh[where, cut, :], cols, NT, preferred_element_type=jnp.float32
        ) + lax.dot_general(sl[where, cut, :], cols, NT, preferred_element_type=jnp.float32)

    def block(s):
        return pl.ds(s * rows, rows)

    def a_copy(s):
        return send(
            part.at[2, block(s), :], ra.at[s], as_.at[s], ar.at[s],
            x_next if s % 2 == 0 else x_prev,
        )

    def x_copy(k, s):
        return send(
            part.at[1 if k == 0 else 3, block(s), :], rx.at[k, block(s), :],
            xs.at[k, s], xr.at[k, s], x_next if k == 0 else x_prev,
        )

    def compute(s):
        for dx in (2, 1, 3, 0):
            @pl.when(active(dx))
            def _():
                if s == 0:
                    c_copy(0, j_ref, dx).wait_recv()
                    c_copy(1, j_ref, dx).wait_recv()
                part[dx, block(s), :] = half_product(0, block(s), columns(0, dx)) + half_product(
                    1, block(s), columns(1, dx)
                )
                if dx == 2:
                    a_copy(s).start()
                if dx == 1 and s % 2 == 1:
                    x_copy(0, s).start()
                if dx == 3 and s % 2 == 0:
                    x_copy(1, s).start()

    def relay(s):
        dx = 1 if s % 2 == 0 else 3

        @pl.when(active(dx))
        def _():
            a_copy(s).wait_recv()
            part[dx, block(s), :] = part[dx, block(s), :] + ra[s]
            x_copy(s % 2, s).start()

    def f_copy(s):
        cut = pl.ds(s * rows, rows)
        device = y_prev if s == 1 else y_next
        return send(fin.at[cut, :], yb.at[s // 2], fs.at[s // 2], fr.at[s // 2], device)

    def g_copy(q, leg):
        src = fin.at[pl.ds(2 * rows + q * half_rows, half_rows), :] if leg == 0 else fb.at[q]
        dst = fb.at[q] if leg == 0 else yb.at[2, pl.ds(q * half_rows, half_rows), :]
        return send(src, dst, gs.at[leg, q], gr.at[leg, q], y_next if q == 0 else y_prev)

    j_own = x * 2 + h
    mine = j_own <= i

    def final(s):
        @pl.when(mine)
        def _():
            x_copy(0, s).wait_recv()
            x_copy(1, s).wait_recv()
            fin[block(s), :] = part[0, block(s), :] + rx[0, block(s), :] + rx[1, block(s), :]
            if s == 2:
                g_copy(0, 0).start()
                g_copy(1, 0).start()
            elif s > 0:
                f_copy(s).start()

    compute(0)
    y_relay(1, 0)
    y_relay(1, 1)
    y_copy(1, 1, 1, j_ref).wait_recv()
    scale(1, 1, rb[0, 1])
    compute(1)
    relay(0)
    for q in (0, 1):
        y_copy(1, q, 2, j_ref).wait_recv()
    scale(1, 2, rb[1, 1])
    compute(2)
    relay(1)
    y_copy(1, 0, 3, j_ref).wait_recv()
    scale(1, 3, rb[2, 1])
    compute(3)
    final(0)
    relay(2)
    final(1)
    relay(3)
    final(2)
    final(3)

    @pl.when(mine)
    def _():
        def place(s, value):
            source = rem(y + s, 4)
            row = ((i * 2 + c) * 4 + y) * rows + lax.broadcasted_iota(jnp.int32, (rows, rows), 0)
            lane = lax.broadcasted_iota(jnp.int32, (rows, rows), 1)
            for k in (0, 1):
                block = (c if k == 0 else 1 - c) * 4 + source
                col = j_own * (rows * 8) + block * rows + lane
                piece = value[:, k * rows:(k + 1) * rows]
                out_ref[:, pl.ds(pl.multiple_of(block * rows, rows), rows)] = jnp.where(
                    col <= row, piece, 0.0
                )

        place(0, fin[0:rows, :])
        for q in (0, 1):
            g_copy(q, 0).wait_recv()
            g_copy(q, 1).start()
        for s in (1, 3):
            f_copy(s).wait_recv()
            place(s, yb[s // 2])
        for q in (0, 1):
            g_copy(q, 1).wait_recv()
        place(2, yb[2])

    @pl.when(j_own > i)
    def _():
        out_ref[...] = jnp.zeros_like(out_ref)

    for k in (0, 1):
        p_copy(k).wait_send()
    for way in (0, 1):
        for d in range(1, 9):
            @pl.when(sends(way, d))
            def _():
                for p in range(pieces):
                    z_copy(way, d, p).wait_send()
    for where in (0, 1):
        for q in (0, 1):
            for s in (1, 2, 3):
                y_copy(where, q, s, j_ref).wait_send()
    for dx in range(4):
        @pl.when(active(dx))
        def _():
            for where in (0, 1):
                c_copy(where, j_ref, dx).wait_send()
            if dx == 2:
                for s in range(4):
                    a_copy(s).wait_send()
            if dx == 1 or dx == 3:
                for s in range(4):
                    x_copy(0 if dx == 1 else 1, s).wait_send()

    @pl.when(mine)
    def _():
        for s in (1, 3):
            f_copy(s).wait_send()
        for q in (0, 1):
            g_copy(q, 0).wait_send()
            g_copy(q, 1).wait_send()


def on_device(pieces, jacobian, extinction, prior_var):
    rows, vox = jacobian.shape
    width = rows * 8
    dma = pltpu.SemaphoreType.DMA
    vmem = pltpu.VMEM
    f32, bf16 = jnp.float32, jnp.bfloat16
    return pl.pallas_call(
        functools.partial(kernel, pieces),
        out_shape=jax.ShapeDtypeStruct((rows, width), f32),
        in_specs=[
            pl.BlockSpec(memory_space=pl.ANY),
            pl.BlockSpec(memory_space=pl.ANY),
            pl.BlockSpec(memory_space=pl.ANY),
        ],
        out_specs=pl.BlockSpec(memory_space=pltpu.VMEM),
        scratch_shapes=[
            vmem((2, 9, rows, vox), bf16),
            vmem((4, 2, rows, vox), bf16),
            vmem((3, 2, rows, vox), bf16),
            vmem((4, 2), f32),
            vmem((3, 2, vox), f32),
            vmem((4, vox), f32),
            vmem((2, rows * 4, vox), bf16),
            vmem((2, rows * 4, vox), bf16),
            vmem((4, rows * 4, rows * 2), f32),
            vmem((4, rows, rows * 2), f32),
            vmem((2, rows * 4, rows * 2), f32),
            vmem((rows * 4, rows * 2), f32),
            vmem((3, rows, rows * 2), f32),
            vmem((2, rows // 2, rows * 2), f32),
            dma((2, 9, pieces)), dma((2, 9, pieces)),
            dma((2, 4)), dma((2, 4)),
            dma((2, 2, 3)), dma((2, 2, 3)),
            dma((4,)), dma((4,)),
            dma((2, 4)), dma((2, 4)),
            dma((2,)), dma((2,)),
            dma((2, 2)), dma((2, 2)),
            dma((2,)), dma((2,)),
            dma((3,)),
        ],
        compiler_params=pltpu.CompilerParams(
            collective_id=0, has_side_effects=True, vmem_limit_bytes=67043328
        ),
    )(jacobian, extinction, prior_var)


def solution(mesh):
    return jax.shard_map(
        functools.partial(on_device, 4),
        mesh=mesh,
        in_specs=(P(("row", "wl"), "vox"), P(), P(None, "vox")),
        out_specs=P(("row", "wl"), "vox"),
        check_vma=False,
    )
```

time: 80.5 us -> 77.9 us (0.968)
  Pallas kernels: 77.1 us -> 74.4 us
    pallas_call x1, Pallas kernels: 77.1 us -> 74.4 us  [on_device(): pl.pallas_call(functools.partial(kernel, pieces), out_shape=jax.ShapeDtyp...]
    unnamed x6 -> x2, local copies, waits for them, and re-layouts: 3.16 us -> 3.22 us
where the time goes in v2:
time: 77.9 us; the launch traced here: 77.7 us
  Pallas kernels  74.4 us (96%)
  local copies, waits for them, and re-layouts  3.22 us (4%)
    pallas_call x1, Pallas kernels, on_device(): pl.pallas_call(functools.partial(kernel, pieces), out_shape=jax.ShapeDtyp...  74.4 us
    unnamed x2, local copies, waits for them, and re-layouts  3.22 us

profile of v2, /device:TPU:64, one launch (start us, length us, event | category | flops | bytes accessed | tf_op | source)
XLA Modules:
  0.0 77.7 jit_solution(4352610974202582935)
XLA Ops:
  0.0 1.3 %copy.4.ext_ref = f32[4,2]{1,0:T(4,128)} copy(f32[4,2]{0,1:T(2,128)} %param.4) | data formatting | bytes 64 | tf_op args[1]
  1.3 74.4 %shard_map.37 = f32[128,1024]{1,0:T(8,128)} custom-call(bf16[128,640]{1,0:T(8,128)(2,1)} %j_ref.1, f32[4,2]{1,0:T(4,128)} %copy.4.ext_ref, f32[2,640]{1,0:T(2,128)} %pri_ref.1), custom_call_target="tpu_custom_call" | custom-call | tf_op jit(solution)/shard_map/pallas_call | solution.py:360
  75.8 1.9 %copy.6 = f32[128,1024]{1,0:T(8,128)} copy(f32[128,1024]{1,0:T(8,128)} %shard_map.37) | data formatting | bytes 1048576

commit v3 on v2

v3 whole, which is shorter than its diff:
```python
import functools
import jax
import jax.numpy as jnp
from jax import lax
from jax.experimental import pallas as pl
from jax.experimental.pallas import tpu as pltpu
from jax.sharding import PartitionSpec as P

MESH = pl.DeviceIdType.MESH
NT = (((1,), (1,)), ((), ()))


def rem(a, n):
    return lax.rem(a, jnp.int32(n))


def div(a, n):
    return lax.div(a, jnp.int32(n))


def kernel(
    pieces,
    j_ref, ext_ref, pri_ref, out_ref,
    zb, cb, rb, ext, pri, tab, sc, part, ra, rx, fin, yb,
    zs, zr, cs, cr, ys, yr, as_, ar, xs, xr, fs, fr, ps, pr, ls,
):
    rows, vox = j_ref.shape
    step = rows // pieces
    half_rows = rows // 2
    v = lax.axis_index("vox")
    r = lax.axis_index("row")
    y = lax.axis_index("wl")
    x, h = div(v, 2), rem(v, 2)
    i, c = div(r, 2), rem(r, 2)
    z = h * 8 + i
    role = rem(i + h, 2)
    kind = rem(i + h + div(i, 7) * c, 2)

    def at(x_=None, z_=None, y_=None, c_=None):
        x_ = x if x_ is None else x_
        z_ = z if z_ is None else z_
        y_ = y if y_ is None else y_
        c_ = c if c_ is None else c_
        return {"vox": x_ * 2 + div(z_, 8), "row": rem(z_, 8) * 2 + c_, "wl": y_}

    x_next, x_prev = at(x_=rem(x + 1, 4)), at(x_=rem(x + 3, 4))
    y_next, y_far, y_prev = (at(y_=rem(y + k, 4)) for k in (1, 2, 3))
    z_next, z_prev = at(z_=rem(z + 1, 16)), at(z_=rem(z + 15, 16))
    z_up, z_down = at(z_=rem(z + 4, 16)), at(z_=rem(z + 12, 16))
    other = at(c_=1 - c)

    barrier = pltpu.get_barrier_semaphore()
    partners = (z_up, z_down, z_next, z_prev, y_far, y_next, y_prev, x_next, x_prev, other)
    for device in partners:
        pl.semaphore_signal(barrier, inc=1, device_id=device, device_id_type=MESH)
    loads = [
        pltpu.make_async_copy(src, dst, ls.at[k])
        for k, (src, dst) in enumerate(((j_ref, zb.at[0, 0]), (ext_ref, ext), (pri_ref, pri.at[0])))
    ]
    for load in loads:
        load.start()
    loads[0].wait()
    pl.semaphore_wait(barrier, len(partners))

    def send(src, dst, ssem, rsem, device):
        return pltpu.make_async_remote_copy(
            src_ref=src, dst_ref=dst, send_sem=ssem, recv_sem=rsem,
            device_id=device, device_id_type=MESH,
        )

    def source(way, d):
        s = rem(z + 16 - d, 16) if way == 0 else rem(z + d, 16)
        place = rem(s, 8)
        return rem(div(s, 8) + place + div(place, 7) * c, 2)

    def has(way, d):
        return source(way, d) == way

    def sends(way, d):
        return source(way, d - 1) == way

    def z_copy(way, d, p):
        cut = pl.ds(p * step, step)
        src = zb.at[0, 0] if d == 1 else zb.at[way, d - 1]
        device = z_next if way == 0 else z_prev
        return send(
            src.at[cut, :], zb.at[way, d, cut, :], zs.at[way, d, p], zr.at[way, d, p], device
        )

    def target(delta):
        return div(i - delta - h, 2)

    def c_copy(where, src, t, q):
        cut = pl.ds(q * half_rows, half_rows)
        return send(
            src.at[cut, :], cb.at[t, where, cut, :], cs.at[where, t, q], cr.at[where, t, q], other
        )

    def y_copy(where, q, s, src):
        cut = pl.ds(q * half_rows, half_rows)
        return send(
            src.at[cut, :], rb.at[s - 1, where, cut, :],
            ys.at[where, q, s - 1], yr.at[where, q, s - 1],
            y_prev if s == 3 or (s == 2 and q == 1) else y_next,
        )

    def y_relay(where, q):
        s = 1 if q == 0 else 3
        y_copy(where, q, s, rb.at[s - 1, where]).wait_recv()
        y_copy(where, q, 2, rb.at[s - 1, where]).start()

    def p_copy(k):
        return send(pri_ref if k == 0 else pri.at[1], pri.at[k + 1], ps.at[k], pr.at[k], z_up)

    def start_z(way, d, p):
        @pl.when(sends(way, d))
        def _():
            z_copy(way, d, p).start()

    for p in range(pieces):
        start_z(0, 1, p)
        start_z(1, 1, p)
    p_copy(0).start()
    for q in (0, 1):
        for s in (1, 3):
            y_copy(0, q, s, zb.at[0, 0]).start()

    @pl.when(role == 0)
    def _():
        for q in (0, 1):
            c_copy(0, zb.at[0, 0], target(0), q).start()

    def take(d):
        for p in range(pieces):
            for way in (0, 1):
                @pl.when(has(way, d))
                def _():
                    z_copy(way, d, p).wait_recv()
                    if d < 8:
                        z_copy(way, d + 1, p).start()
                    if (p + 1) % (pieces // 2) != 0:
                        return
                    q = (p + 1) // (pieces // 2) - 1
                    chunk = zb.at[way, d]
                    if d < 8:
                        delta = d if way == 0 else 8 - d

                        @pl.when((delta <= i) & (rem(i + h + delta, 2) == 0))
                        def _():
                            c_copy(way, chunk, target(delta), q).start()
                    else:
                        y_copy(1, q, 1, chunk).start()
                        y_copy(1, q, 3, chunk).start()

                        @pl.when(role == 0)
                        def _():
                            c_copy(1, chunk, target(0), q).start()

    for d in (1, 2, 3):
        take(d)
    y_relay(0, 0)
    y_relay(0, 1)
    p_copy(0).wait_recv()
    p_copy(1).start()
    for d in (4, 5):
        take(d)

    def weigh(where):
        lane = lax.broadcasted_iota(jnp.int32, (2, 4), 1)
        values = ext[...]
        both = values * jnp.sum(jnp.where(lane == y, values, 0.0), axis=1, keepdims=True)
        own = pri[where * 2]
        for a in range(4):
            tab[a:a + 1, :] = both[0:1, a:a + 1] * own[0:1, :] + both[1:2, a:a + 1] * own[1:2, :]

    def scale(where, s, src, high_at, low_at):
        value = src.astype(jnp.float32) * tab[pl.ds(rem(y + 4 - s, 4), 1), :]
        high = value.astype(jnp.bfloat16)
        count = src.shape[0]
        sc[where, high_at:high_at + count, :] = high
        sc[where, low_at:low_at + count, :] = (value - high.astype(jnp.float32)).astype(jnp.bfloat16)

    def scale_own(s, src):
        scale(0, s, src, s * rows, (4 + s) * rows)

    def scale_far(b, src):
        scale(1, b // 2, src, b * rows, b * rows + half_rows)

    def active(t):
        return t * 2 + h <= i

    def columns(where, t):
        delta = i - t * 2 - h
        if where == 0:
            own = zb[0, delta]
        else:
            own = zb[jnp.where(delta == 0, 1 - kind, 1), 8 - delta]
        return jnp.concatenate([own, cb[t, where]], axis=0)

    def block(b):
        return pl.ds(b * half_rows, half_rows)

    far_x = rem(x + 2, 4)
    sides = (rem(x + 1, 4), rem(x + 3, 4))

    def a_copy(b):
        return send(
            part.at[far_x, block(b), :], ra.at[b], as_.at[b], ar.at[b],
            x_next if b % 2 == 0 else x_prev,
        )

    def x_copy(k, b):
        return send(
            part.at[sides[k], block(b), :], rx.at[k, block(b), :],
            xs.at[k, b], xr.at[k, b], x_next if k == 0 else x_prev,
        )

    def own_half():
        for t in range(4):
            @pl.when(active(t))
            def _():
                for q in (0, 1):
                    c_copy(0, j_ref, t, q).wait_recv()
                both = lax.dot_general(
                    sc[0], columns(0, t), NT, preferred_element_type=jnp.float32
                )
                part[t] = both[:rows * 4] + both[rows * 4:]

    def compute(b):
        for t in range(4):
            @pl.when(active(t))
            def _():
                if b == 0:
                    for q in (0, 1):
                        c_copy(1, j_ref, t, q).wait_recv()
                both = lax.dot_general(
                    sc[1, b * rows:(b + 1) * rows, :], columns(1, t), NT,
                    preferred_element_type=jnp.float32,
                )
                part[t, block(b), :] = part[t, block(b), :] + (both[:half_rows] + both[half_rows:])

                @pl.when(far_x == t)
                def _():
                    a_copy(b).start()

                @pl.when(sides[1 - b % 2] == t)
                def _():
                    x_copy(1 - b % 2, b).start()

    def relay(b):
        k = b % 2

        @pl.when(active(sides[k]))
        def _():
            a_copy(b).wait_recv()
            part[sides[k], block(b), :] = part[sides[k], block(b), :] + ra[b]
            x_copy(k, b).start()

    def f_copy(b):
        device = (None, y_prev, y_far, y_next)[b // 2]
        return send(fin.at[block(b), :], yb.at[block(b), :], fs.at[b], fr.at[b], device)

    j_own = x * 2 + h
    mine = j_own <= i

    def final(b):
        @pl.when(mine)
        def _():
            x_copy(0, b).wait_recv()
            x_copy(1, b).wait_recv()
            fin[block(b), :] = part[x, block(b), :] + rx[0, block(b), :] + rx[1, block(b), :]
            if b // 2 != 0:
                f_copy(b).start()

    for q in (0, 1):
        y_copy(0, q, 1 if q == 1 else 3, j_ref).wait_recv()
        y_copy(0, q, 2, j_ref).wait_recv()
    for load in loads[1:]:
        load.wait()
    weigh(0)
    scale_own(0, zb[0, 0])
    for s in (1, 2, 3):
        scale_own(s, rb[s - 1, 0])
    for d in (6, 7):
        take(d)
    own_half()
    p_copy(1).wait_recv()
    weigh(1)

    take(8)

    def arrived(b):
        s, q = b // 2, b % 2
        if s == 0:
            src = zb[1 - kind, 8, q * half_rows:(q + 1) * half_rows, :]
        else:
            src = rb[s - 1, 1, q * half_rows:(q + 1) * half_rows, :]
        scale_far(b, src)
        compute(b)

    arrived(0)
    arrived(1)
    y_relay(1, 0)
    arrived(2)
    y_relay(1, 1)
    arrived(7)
    y_copy(1, 1, 1, j_ref).wait_recv()
    arrived(3)
    relay(0)
    relay(1)
    y_copy(1, 0, 3, j_ref).wait_recv()
    arrived(6)
    y_copy(1, 0, 2, j_ref).wait_recv()
    arrived(4)
    y_copy(1, 1, 2, j_ref).wait_recv()
    arrived(5)
    relay(2)
    relay(7)
    relay(3)
    relay(6)
    final(0)
    final(1)
    final(2)
    final(7)
    relay(4)
    relay(5)
    final(3)
    final(6)
    final(4)
    final(5)

    @pl.when(mine)
    def _():
        def place(s, value):
            source = rem(y + s, 4)
            row = ((i * 2 + c) * 4 + y) * rows + lax.broadcasted_iota(jnp.int32, (rows, rows), 0)
            lane = lax.broadcasted_iota(jnp.int32, (rows, rows), 1)
            for k in (0, 1):
                block = (c if k == 0 else 1 - c) * 4 + source
                col = j_own * (rows * 8) + block * rows + lane
                piece = value[:, k * rows:(k + 1) * rows]
                out_ref[:, pl.ds(pl.multiple_of(block * rows, rows), rows)] = jnp.where(
                    col <= row, piece, 0.0
                )

        place(0, fin[0:rows, :])
        for s in (1, 3, 2):
            for q in (0, 1):
                f_copy(s * 2 + q).wait_recv()
            place(s, yb[s * rows:(s + 1) * rows, :])

    @pl.when(j_own > i)
    def _():
        out_ref[...] = jnp.zeros_like(out_ref)

    for k in (0, 1):
        p_copy(k).wait_send()
    for way in (0, 1):
        for d in range(1, 9):
            @pl.when(sends(way, d))
            def _():
                for p in range(pieces):
                    z_copy(way, d, p).wait_send()
    for where in (0, 1):
        for q in (0, 1):
            for s in (1, 2, 3):
                y_copy(where, q, s, j_ref).wait_send()
    for t in range(4):
        @pl.when(active(t))
        def _():
            for where in (0, 1):
                for q in (0, 1):
                    c_copy(where, j_ref, t, q).wait_send()

    @pl.when(active(far_x))
    def _():
        for b in range(8):
            a_copy(b).wait_send()
    for k in (0, 1):
        @pl.when(active(sides[k]))
        def _():
            for b in range(8):
                x_copy(k, b).wait_send()

    @pl.when(mine)
    def _():
        for b in range(2, 8):
            f_copy(b).wait_send()


def on_device(pieces, jacobian, extinction, prior_var):
    rows, vox = jacobian.shape
    width = rows * 8
    dma = pltpu.SemaphoreType.DMA
    vmem = pltpu.VMEM
    f32, bf16 = jnp.float32, jnp.bfloat16
    return pl.pallas_call(
        functools.partial(kernel, pieces),
        out_shape=jax.ShapeDtypeStruct((rows, width), f32),
        in_specs=[
            pl.BlockSpec(memory_space=pl.ANY),
            pl.BlockSpec(memory_space=pl.ANY),
            pl.BlockSpec(memory_space=pl.ANY),
        ],
        out_specs=pl.BlockSpec(memory_space=pltpu.VMEM),
        scratch_shapes=[
            vmem((2, 9, rows, vox), bf16),
            vmem((4, 2, rows, vox), bf16),
            vmem((3, 2, rows, vox), bf16),
            vmem((2, 4), f32),
            vmem((3, 2, vox), f32),
            vmem((4, vox), f32),
            vmem((2, rows * 8, vox), bf16),
            vmem((4, rows * 4, rows * 2), f32),
            vmem((8, rows // 2, rows * 2), f32),
            vmem((2, rows * 4, rows * 2), f32),
            vmem((rows * 4, rows * 2), f32),
            vmem((rows * 4, rows * 2), f32),
            dma((2, 9, pieces)), dma((2, 9, pieces)),
            dma((2, 4, 2)), dma((2, 4, 2)),
            dma((2, 2, 3)), dma((2, 2, 3)),
            dma((8,)), dma((8,)),
            dma((2, 8)), dma((2, 8)),
            dma((8,)), dma((8,)),
            dma((2,)), dma((2,)),
            dma((3,)),
        ],
        compiler_params=pltpu.CompilerParams(
            collective_id=0, has_side_effects=True, vmem_limit_bytes=67043328
        ),
    )(jacobian, extinction.T, prior_var)


def solution(mesh):
    return jax.shard_map(
        functools.partial(on_device, 4),
        mesh=mesh,
        in_specs=(P(("row", "wl"), "vox"), P(), P(None, "vox")),
        out_specs=P(("row", "wl"), "vox"),
        check_vma=False,
    )
```

time: 77.9 us -> 75 us (0.963)
  Pallas kernels: 74.4 us -> 72.6 us
  local copies, waits for them, and re-layouts: 3.22 us -> 1.89 us
    pallas_call x1, Pallas kernels: 74.4 us -> 72.6 us  [on_device(): pl.pallas_call(functools.partial(kernel, pieces), out_shape=jax.ShapeDtyp...]
    unnamed x2 -> x1, local copies, waits for them, and re-layouts: 3.22 us -> 1.89 us
where the time goes in v3:
time: 75 us; the launch traced here: 74.5 us
  Pallas kernels  72.6 us (97%)
  local copies, waits for them, and re-layouts  1.89 us (3%)
    pallas_call x1, Pallas kernels, on_device(): pl.pallas_call(functools.partial(kernel, pieces), out_shape=jax.ShapeDtyp...  72.6 us
    unnamed x1, local copies, waits for them, and re-layouts  1.89 us

profile of v3, /device:TPU:64, one launch (start us, length us, event | category | flops | bytes accessed | tf_op | source)
XLA Modules:
  0.0 74.5 jit_solution(17411731706043907866)
XLA Ops:
  0.0 72.6 %shard_map.37 = f32[128,1024]{1,0:T(8,128)} custom-call(bf16[128,640]{1,0:T(8,128)(2,1)} %j_ref.1, f32[2,4]{1,0:T(2,128)} %bitcast.1, f32[2,640]{1,0:T(2,128)} %pri_ref.1), custom_call_target="tpu_custom_call" | custom-call | tf_op jit(solution)/shard_map/pallas_call | solution.py:397
  72.6 1.9 %copy.5 = f32[128,1024]{1,0:T(8,128)} copy(f32[128,1024]{1,0:T(8,128)} %shard_map.37) | data formatting | bytes 1048576

commit v4 on v3

--- a/solution.py
+++ b/solution.py
@@ -21,8 +21,8 @@
 def kernel(
     pieces,
     j_ref, ext_ref, pri_ref, out_ref,
-    zb, cb, rb, ext, pri, tab, sc, part, ra, rx, fin, yb,
-    zs, zr, cs, cr, ys, yr, as_, ar, xs, xr, fs, fr, ps, pr, ls,
+    zb, rb, ext, pri, tab, sc, part, ra, rx, fin, yb,
+    zs, zr, cs, cr, es, er, ys, yr, as_, ar, xs, xr, fs, fr, ps, pr, ls,
 ):
     rows, vox = j_ref.shape
     step = rows // pieces
@@ -35,6 +35,7 @@
     z = h * 8 + i
     role = rem(i + h, 2)
     kind = rem(i + h + div(i, 7) * c, 2)
+    kind_other = rem(i + h + div(i, 7) * (1 - c), 2)
 
     def at(x_=None, z_=None, y_=None, c_=None):
         x_ = x if x_ is None else x_
@@ -55,7 +56,7 @@
         pl.semaphore_signal(barrier, inc=1, device_id=device, device_id_type=MESH)
     loads = [
         pltpu.make_async_copy(src, dst, ls.at[k])
-        for k, (src, dst) in enumerate(((j_ref, zb.at[0, 0]), (ext_ref, ext), (pri_ref, pri.at[0])))
+        for k, (src, dst) in enumerate(((j_ref, zb.at[c, 0, 0]), (ext_ref, ext), (pri_ref, pri.at[0])))
     ]
     for load in loads:
         load.start()
@@ -68,33 +69,42 @@
             device_id=device, device_id_type=MESH,
         )
 
-    def source(way, d):
+    def source(k, way, d):
         s = rem(z + 16 - d, 16) if way == 0 else rem(z + d, 16)
         place = rem(s, 8)
-        return rem(div(s, 8) + place + div(place, 7) * c, 2)
-
-    def has(way, d):
-        return source(way, d) == way
-
-    def sends(way, d):
-        return source(way, d - 1) == way
-
-    def z_copy(way, d, p):
+        return rem(div(s, 8) + place + (div(place, 7) if k else 0), 2)
+
+    def has(k, way, d):
+        return source(k, way, d) == way
+
+    def sends(k, way, d):
+        return source(k, way, d - 1) == way
+
+    def z_copy(k, way, d, p):
         cut = pl.ds(p * step, step)
-        src = zb.at[0, 0] if d == 1 else zb.at[way, d - 1]
+        src = zb.at[k, 0, 0] if d == 1 else zb.at[k, way, d - 1]
         device = z_next if way == 0 else z_prev
         return send(
-            src.at[cut, :], zb.at[way, d, cut, :], zs.at[way, d, p], zr.at[way, d, p], device
+            src.at[cut, :], zb.at[k, way, d, cut, :], zs.at[k, way, d, p], zr.at[k, way, d, p], device
         )
 
-    def target(delta):
-        return div(i - delta - h, 2)
-
-    def c_copy(where, src, t, q):
+    def c_copy(k, way, d, q):
         cut = pl.ds(q * half_rows, half_rows)
-        return send(
-            src.at[cut, :], cb.at[t, where, cut, :], cs.at[where, t, q], cr.at[where, t, q], other
-        )
+        place = zb.at[k, way, d, cut, :]
+        return send(place, place, cs.at[k, way, d, q], cr.at[k, way, d, q], other)
+
+    def column_at(delta, way):
+        return (delta >= 0) & (delta <= i) & (rem(i + h + delta, 2) == 0)
+
+    def handed(k, way, d):
+        if d == 8:
+            return has(k, way, d) if k == 0 else has(k, way, d) & (role == 0)
+        return has(k, way, d) & column_at(d if way == 0 else 8 - d, way)
+
+    def e_copy():
+        return send(zb.at[c, 0, 0], zb.at[c, 0, 0], es, er, other)
+
+    first, second = c == 0, c == 1
 
     def y_copy(where, q, s, src):
         cut = pl.ds(q * half_rows, half_rows)
@@ -112,49 +122,47 @@
     def p_copy(k):
         return send(pri_ref if k == 0 else pri.at[1], pri.at[k + 1], ps.at[k], pr.at[k], z_up)
 
-    def start_z(way, d, p):
-        @pl.when(sends(way, d))
-        def _():
-            z_copy(way, d, p).start()
-
-    for p in range(pieces):
-        start_z(0, 1, p)
-        start_z(1, 1, p)
+    e_copy().start()
+
+    def start_z(k):
+        for p in range(pieces):
+            for way in (0, 1):
+                @pl.when(second & sends(k, way, 1))
+                def _():
+                    z_copy(k, way, 1, p).start()
+
+    start_z(1)
     p_copy(0).start()
     for q in (0, 1):
         for s in (1, 3):
-            y_copy(0, q, s, zb.at[0, 0]).start()
-
-    @pl.when(role == 0)
-    def _():
-        for q in (0, 1):
-            c_copy(0, zb.at[0, 0], target(0), q).start()
+            y_copy(0, q, s, zb.at[c, 0, 0]).start()
+
+    e_copy().wait_recv()
+    start_z(0)
+
+    def y_start(src, q):
+        y_copy(1, q, 1, src).start()
+        y_copy(1, q, 3, src).start()
 
     def take(d):
+        def move(k, way, p):
+            z_copy(k, way, d, p).wait_recv()
+            if d < 8:
+                z_copy(k, way, d + 1, p).start()
+            if (p + 1) % (pieces // 2) != 0:
+                return
+            q = (p + 1) // (pieces // 2) - 1
+            if d == 8 and k == 1:
+                y_start(zb.at[k, way, d], q)
+
+            @pl.when(handed(k, way, d))
+            def _():
+                c_copy(k, way, d, q).start()
+
         for p in range(pieces):
-            for way in (0, 1):
-                @pl.when(has(way, d))
-                def _():
-                    z_copy(way, d, p).wait_recv()
-                    if d < 8:
-                        z_copy(way, d + 1, p).start()
-                    if (p + 1) % (pieces // 2) != 0:
-                        return
-                    q = (p + 1) // (pieces // 2) - 1
-                    chunk = zb.at[way, d]
-                    if d < 8:
-                        delta = d if way == 0 else 8 - d
-
-                        @pl.when((delta <= i) & (rem(i + h + delta, 2) == 0))
-                        def _():
-                            c_copy(way, chunk, target(delta), q).start()
-                    else:
-                        y_copy(1, q, 1, chunk).start()
-                        y_copy(1, q, 3, chunk).start()
-
-                        @pl.when(role == 0)
-                        def _():
-                            c_copy(1, chunk, target(0), q).start()
+            for k in (1, 0):
+                for way in (0, 1):
+                    pl.when(second & has(k, way, d))(functools.partial(move, k, way, p))
 
     for d in (1, 2, 3):
         take(d)
@@ -192,10 +200,32 @@
     def columns(where, t):
         delta = i - t * 2 - h
         if where == 0:
-            own = zb[0, delta]
+            pair = zb[c, 0, delta], zb[1 - c, 0, delta]
         else:
-            own = zb[jnp.where(delta == 0, 1 - kind, 1), 8 - delta]
-        return jnp.concatenate([own, cb[t, where]], axis=0)
+            at_end = delta == 0
+            pair = (
+                zb[c, jnp.where(at_end, 1 - kind, 1), 8 - delta],
+                zb[1 - c, jnp.where(at_end, 1 - kind_other, 1), 8 - delta],
+            )
+        return jnp.concatenate(pair, axis=0)
+
+    def taken(where, t):
+        delta = i - t * 2 - h
+        for k in (0, 1):
+            for q in (0, 1):
+                if where == 0:
+                    @pl.when(first & (delta > 0))
+                    def _():
+                        c_copy(k, 0, delta, q).wait_recv()
+                else:
+                    @pl.when(first & (delta > 0))
+                    def _():
+                        c_copy(k, 1, 8 - delta, q).wait_recv()
+        if where == 1:
+            @pl.when(first & (delta == 0))
+            def _():
+                for q in (0, 1):
+                    c_copy(1, 1 - kind_other, 8, q).wait_recv()
 
     def block(b):
         return pl.ds(b * half_rows, half_rows)
@@ -219,8 +249,7 @@
         for t in range(4):
             @pl.when(active(t))
             def _():
-                for q in (0, 1):
-                    c_copy(0, j_ref, t, q).wait_recv()
+                taken(0, t)
                 both = lax.dot_general(
                     sc[0], columns(0, t), NT, preferred_element_type=jnp.float32
                 )
@@ -231,8 +260,7 @@
             @pl.when(active(t))
             def _():
                 if b == 0:
-                    for q in (0, 1):
-                        c_copy(1, j_ref, t, q).wait_recv()
+                    taken(1, t)
                 both = lax.dot_general(
                     sc[1, b * rows:(b + 1) * rows, :], columns(1, t), NT,
                     preferred_element_type=jnp.float32,
@@ -278,7 +306,7 @@
     for load in loads[1:]:
         load.wait()
     weigh(0)
-    scale_own(0, zb[0, 0])
+    scale_own(0, zb[c, 0, 0])
     for s in (1, 2, 3):
         scale_own(s, rb[s - 1, 0])
     for d in (6, 7):
@@ -288,11 +316,16 @@
     weigh(1)
 
     take(8)
+    for q in (0, 1):
+        @pl.when(first)
+        def _():
+            c_copy(0, 1 - kind, 8, q).wait_recv()
+            y_start(zb.at[0, 1 - kind, 8], q)
 
     def arrived(b):
         s, q = b // 2, b % 2
         if s == 0:
-            src = zb[1 - kind, 8, q * half_rows:(q + 1) * half_rows, :]
+            src = zb[c, 1 - kind, 8, q * half_rows:(q + 1) * half_rows, :]
         else:
             src = rb[s - 1, 1, q * half_rows:(q + 1) * half_rows, :]
         scale_far(b, src)
@@ -355,23 +388,23 @@
 
     for k in (0, 1):
         p_copy(k).wait_send()
-    for way in (0, 1):
-        for d in range(1, 9):
-            @pl.when(sends(way, d))
-            def _():
-                for p in range(pieces):
-                    z_copy(way, d, p).wait_send()
+    e_copy().wait_send()
+    for k in (0, 1):
+        for way in (0, 1):
+            for d in range(1, 9):
+                @pl.when(second & sends(k, way, d))
+                def _():
+                    for p in range(pieces):
+                        z_copy(k, way, d, p).wait_send()
+
+                @pl.when(second & handed(k, way, d))
+                def _():
+                    for q in (0, 1):
+                        c_copy(k, way, d, q).wait_send()
     for where in (0, 1):
         for q in (0, 1):
             for s in (1, 2, 3):
                 y_copy(where, q, s, j_ref).wait_send()
-    for t in range(4):
-        @pl.when(active(t))
-        def _():
-            for where in (0, 1):
-                for q in (0, 1):
-                    c_copy(where, j_ref, t, q).wait_send()
-
     @pl.when(active(far_x))
     def _():
         for b in range(8):
@@ -404,8 +437,7 @@
         ],
         out_specs=pl.BlockSpec(memory_space=pltpu.VMEM),
         scratch_shapes=[
-            vmem((2, 9, rows, vox), bf16),
-            vmem((4, 2, rows, vox), bf16),
+            vmem((2, 2, 9, rows, vox), bf16),
             vmem((3, 2, rows, vox), bf16),
             vmem((2, 4), f32),
             vmem((3, 2, vox), f32),
@@ -416,8 +448,9 @@
             vmem((2, rows * 4, rows * 2), f32),
             vmem((rows * 4, rows * 2), f32),
             vmem((rows * 4, rows * 2), f32),
-            dma((2, 9, pieces)), dma((2, 9, pieces)),
-            dma((2, 4, 2)), dma((2, 4, 2)),
+            dma((2, 2, 9, pieces)), dma((2, 2, 9, pieces)),
+            dma((2, 2, 9, 2)), dma((2, 2, 9, 2)),
+            dma, dma,
             dma((2, 2, 3)), dma((2, 2, 3)),
             dma((8,)), dma((8,)),
             dma((2, 8)), dma((2, 8)),

time: 75 us -> 72.8 us (0.971)
  the two profiles are of different devices: /device:TPU:64 before, /device:TPU:66 now
where the time goes in v4:
time: 72.8 us; the launch traced here: 72.6 us
  Pallas kernels  70.7 us (97%)
  local copies, waits for them, and re-layouts  1.89 us (3%)
    pallas_call x1, Pallas kernels, on_device(): pl.pallas_call(functools.partial(kernel, pieces), out_shape=jax.ShapeDtyp...  70.7 us
    unnamed x1, local copies, waits for them, and re-layouts  1.89 us

profile of v4, /device:TPU:66, one launch (start us, length us, event | category | flops | bytes accessed | tf_op | source)
XLA Modules:
  0.0 72.6 jit_solution(12775956229459510119)
XLA Ops:
  0.0 70.7 %shard_map.37 = f32[128,1024]{1,0:T(8,128)} custom-call(bf16[128,640]{1,0:T(8,128)(2,1)} %j_ref.1, f32[2,4]{1,0:T(2,128)} %bitcast.1, f32[2,640]{1,0:T(2,128)} %pri_ref.1), custom_call_target="tpu_custom_call" | custom-call | tf_op jit(solution)/shard_map/pallas_call | solution.py:430
  70.7 1.9 %copy.5 = f32[128,1024]{1,0:T(8,128)} copy(f32[128,1024]{1,0:T(8,128)} %shard_map.37) | data formatting | bytes 1048576

commit v5 on v4

--- a/solution.py
+++ b/solution.py
@@ -339,10 +339,10 @@
     arrived(7)
     y_copy(1, 1, 1, j_ref).wait_recv()
     arrived(3)
+    y_copy(1, 0, 3, j_ref).wait_recv()
+    arrived(6)
     relay(0)
     relay(1)
-    y_copy(1, 0, 3, j_ref).wait_recv()
-    arrived(6)
     y_copy(1, 0, 2, j_ref).wait_recv()
     arrived(4)
     y_copy(1, 1, 2, j_ref).wait_recv()
@@ -351,14 +351,14 @@
     relay(7)
     relay(3)
     relay(6)
+    relay(4)
+    relay(5)
+    final(2)
+    final(7)
+    final(3)
+    final(6)
     final(0)
     final(1)
-    final(2)
-    final(7)
-    relay(4)
-    relay(5)
-    final(3)
-    final(6)
     final(4)
     final(5)
 
@@ -466,7 +466,7 @@
 
 def solution(mesh):
     return jax.shard_map(
-        functools.partial(on_device, 4),
+        functools.partial(on_device, 2),
         mesh=mesh,
         in_specs=(P(("row", "wl"), "vox"), P(), P(None, "vox")),
         out_specs=P(("row", "wl"), "vox"),

time: 72.8 us -> 71.6 us (0.984)
  the two profiles are of different devices: /device:TPU:66 before, /device:TPU:64 now
where the time goes in v5:
time: 71.6 us; the launch traced here: 71.4 us
  Pallas kernels  69.5 us (97%)
  local copies, waits for them, and re-layouts  1.89 us (3%)
    pallas_call x1, Pallas kernels, on_device(): pl.pallas_call(functools.partial(kernel, pieces), out_shape=jax.ShapeDtyp...  69.5 us
    unnamed x1, local copies, waits for them, and re-layouts  1.89 us

profile of v5, /device:TPU:64, one launch (start us, length us, event | category | flops | bytes accessed | tf_op | source)
XLA Modules:
  0.0 71.4 jit_solution(1055669149391767267)
XLA Ops:
  0.0 69.5 %shard_map.37 = f32[128,1024]{1,0:T(8,128)} custom-call(bf16[128,640]{1,0:T(8,128)(2,1)} %j_ref.1, f32[2,4]{1,0:T(2,128)} %bitcast.1, f32[2,640]{1,0:T(2,128)} %pri_ref.1), custom_call_target="tpu_custom_call" | custom-call | tf_op jit(solution)/shard_map/pallas_call | solution.py:430
  69.5 1.9 %copy.5 = f32[128,1024]{1,0:T(8,128)} copy(f32[128,1024]{1,0:T(8,128)} %shard_map.37) | data formatting | bytes 1048576
